TPU v7x, 128 devices: a whole 4x4x4 slice. The times are simulated.
128 devices in a mesh: row: 8 (over z, core), col: 16 (over y, x).
Axes of the slice: x: 4, y: 4, z: 4, core: 2. Of those that a mesh axis runs over, the one named last changes fastest.
Arguments:
- panel_blocks: bfloat16 [16, 8, 512, 512], P('col', None, 'row'), may hold values from -0.25 to 0.25
- factor_inverse: bfloat16 [16, 512, 512], P('col')
- target_rows: int32 [16, 8], replicated, may hold values from 0 to 15, as said below
- owner_order: int32 [16], replicated, may hold values from 0 to 15, each once
- ancestor_rows: float32 [16, 512, 8192], P('col', 'row'), may hold values from -1.8 to 1.8
Outputs:
- updated_rows: float32 [16, 512, 8192], P('col', 'row')
Inputs may be any that keep to these rules, and one draw needn't show every extreme that they name: `target_rows`: each row names 8 different ancestor block rows in ascending order; each index of col holds exactly one supernode. `owner_order`: each ancestor block row once.
All inputs are finite; a program needn't handle non-finite values.
Results may differ from a plain program's by a relative error of at most 0.0024.
Values may be sent and summed in bfloat16 or wider, within the bound.
A program may use at most 192 MiB of HBM per device.

v0:
```python
import jax
import jax.numpy as jnp
from jax import lax
from jax.sharding import PartitionSpec as P


def body(panel_blocks, factor_inverse, target_rows, owner_order, ancestor_rows):
    col_size = lax.axis_size("col")
    width = panel_blocks.shape[3]
    ancestors = owner_order.shape[0]
    col_place = lax.axis_index("col")
    own_targets = lax.dynamic_slice_in_dim(target_rows, col_place, 1, 0)[0]
    own_solved = jnp.einsum(
        "piw,vw->piv", panel_blocks[0], factor_inverse[0], preferred_element_type=jnp.float32
    ).astype(jnp.bfloat16)
    full_solved = lax.all_gather(own_solved, "row", axis=1, tiled=True)
    products = jnp.einsum(
        "piw,qmw->piqm", own_solved, full_solved, preferred_element_type=jnp.float32
    ).astype(jnp.bfloat16)
    matched = own_targets[None, :] == owner_order[:, None]
    places = lax.broadcasted_iota(jnp.int32, matched.shape, 1)
    position = jnp.sum(jnp.where(matched, places, 0), axis=1)
    present = jnp.any(matched, axis=1)
    send = jnp.where(
        present[:, None, None, None], products[position], jnp.zeros((), products.dtype)
    )
    received = lax.all_to_all(send, "col", 0, 0, tiled=True)
    block_ids = lax.broadcasted_iota(jnp.int32, (1, 1, ancestors), 2)
    onehot = (target_rows[:, :, None] == block_ids).astype(jnp.bfloat16)
    update = jnp.einsum("sqb,siqm->ibm", onehot, received, preferred_element_type=jnp.float32)
    return ancestor_rows - update.reshape(ancestor_rows.shape)


def solution(mesh):
    return jax.shard_map(
        body,
        mesh=mesh,
        in_specs=(
            P("col", None, "row", None),
            P("col", None, None),
            P(),
            P(),
            P("col", "row", None),
        ),
        out_specs=P("col", "row", None),
        check_vma=False,
    )
```

profile of v0, /device:TPU:1, one launch (start us, length us, event | category | flops | bytes accessed | tf_op | source)
XLA Modules:
  0.0 218.7 jit_solution(13225717698894345203)
XLA Ops:
  6.5 0.0 copy-start
  6.5 0.0 all-gather.2.cloned.1.call-start
  6.5 1.0 copy-done
  7.6 2.3 %convolution_convert_fusion = bf16[8,64,512]{2,1,0:T(8,128)(2,1)} fusion(bf16[1,512,512]{2,1,0:T(8,128)(2,1)S(1)} %copy-done, bf16[1,8,64,512]{3,2,1,0:T(8,128)(2,1)} %param.5), kind=kOutput, calls=%fused_computation.6 | convolution fusion | flops 268697600 | bytes 1572864 | tf_op jit(solution)/shard_map/piw,vw->piv/dot_general | solution.py:13
  9.9 0.0 all-gather.2.cloned.1.call-update
  9.9 0.9 dynamic-slice_reduce_fusion
  10.8 0.7 fusion.11
  11.5 0.7 compare_reduce_fusion
  12.3 33.7 %all-gather.2.cloned.1.call-done = bf16[8,512,512]{2,1,0:T(8,128)(2,1)} async-done(((bf16[8,64,512]{2,1,0:T(8,128)(2,1)}), bf16[8,512,512]{2,1,0:T(8,128)(2,1)}) %all-gather.2.cloned.1.call-update) | async-done | bytes 4194320 | tf_op jit(solution)/shard_map/all_gather | solution.py:16
  46.0 4.7 %fusion.2 = bf16[8,64,8,512]{3,1,2,0:T(8,128)(2,1)S(1)} fusion(bf16[8,512,512]{2,1,0:T(8,128)(2,1)} %all-gather.2.cloned.1.call-done, bf16[8,64,512]{2,1,0:T(8,128)(2,1)} %convolution_convert_fusion), kind=kOutput, calls=%fused_computation.4 | convolution fusion | flops 2149580800 | bytes 8912896 | tf_op jit(solution)/shard_map/piw,qmw->piqm/dot_general | solution.py:17
  50.8 4.5 %copy.9 = bf16[8,64,8,512]{3,2,1,0:T(8,128)(2,1)} copy(bf16[8,64,8,512]{3,1,2,0:T(8,128)(2,1)S(1)} %fusion.2) | data formatting | bytes 8388608 | tf_op jit(solution)/shard_map/convert_element_type | solution.py:19
  55.2 6.9 %gather_fusion = bf16[16,64,8,512]{3,2,1,0:T(8,128)(2,1)} fusion(bf16[8,64,8,512]{3,2,1,0:T(8,128)(2,1)} %copy.9, s32[1024]{0:T(1024)S(1)} %pad_clamp_fusion), kind=kCustom, calls=%fused_computation | custom fusion | bytes 16777280 | tf_op jit(solution)/shard_map/gather | solution.py:25
  62.1 7.2 %broadcast_select_fusion = bf16[16,64,8,512]{3,2,1,0:T(8,128)(2,1)} fusion(bf16[16,64,8,512]{3,2,1,0:T(8,128)(2,1)} %gather_fusion, pred[16]{0:T(512)(128)(4,1)S(1)} %compare_reduce_fusion), kind=kLoop, calls=%fused_computation.1 | loop fusion | flops 4194304 | bytes 16777232 | tf_op jit(solution)/shard_map/jit(_where)/select_n | solution.py:24
  69.3 0.0 copy-start.1
  69.3 6.7 %all-to-all-start = ((bf16[16,64,8,512]{3,2,1,0:T(8,128)(2,1)}), bf16[16,64,8,512]{3,2,1,0:T(8,128)(2,1)}, u32[]{:S(2)}, u32[]{:S(2)}) async-start(bf16[16,64,8,512]{3,2,1,0:T(8,128)(2,1)} %broadcast_select_fusion), calls=%async_computation | async-start | bytes 16777216 | tf_op jit(solution)/shard_map/all_to_all | solution.py:27
  76.0 0.0 copy-done.1
  76.0 0.1 copy.10
  76.1 124.9 %all-to-all-done = bf16[16,64,8,512]{3,2,1,0:T(8,128)(2,1)} async-done(((bf16[16,64,8,512]{3,2,1,0:T(8,128)(2,1)}), bf16[16,64,8,512]{3,2,1,0:T(8,128)(2,1)}, u32[]{:S(2)}, u32[]{:S(2)}) %all-to-all-start) | async-done | bytes 8388640 | tf_op jit(solution)/shard_map/all_to_all | solution.py:27
  201.0 6.0 %convolution_bitcast_fusion = f32[64,16,512]{2,1,0:T(8,128)} fusion(bf16[16,64,8,512]{3,2,1,0:T(8,128)(2,1)} %all-to-all-done, s32[16,8]{1,0:T(8,128)S(1)} %copy.10), kind=kOutput, calls=%fused_computation.5 | convolution fusion | flops 134219776 | bytes 10486272 | tf_op jit(solution)/shard_map/sqb,siqm->ibm/dot_general | solution.py:30
  207.0 1.7 reshape.19
  208.7 3.1 %sub.3 = f32[1,64,8192]{2,1,0:T(8,128)} subtract(f32[1,64,8192]{2,1,0:T(8,128)} %param.9, f32[1,64,8192]{2,1,0:T(8,128)S(1)} %reshape.19) | non-fusion elementwise | flops 524288 | bytes 6291456 | tf_op jit(solution)/shard_map/sub | solution.py:31
  (2 shorter events, 0.0 us)
Async XLA Ops:
  6.5 1.0 copy-start
  6.5 39.5 %all-gather.2.cloned.1.call-start = ((), (), s32[]{:S(2)}) async-start(), calls=%async_computation.1 | async-start | bytes 4718592 | tf_op jit(solution)/shard_map/all_gather | solution.py:16
  69.3 6.7 %copy-start.1 = (s32[16,8]{0,1:T(8,128)S(1)}, s32[16,8]{0,1:T(8,128)}, u32[]{:S(2)}) copy-start(s32[16,8]{0,1:T(8,128)} %param.7) | copy-start | bytes 1540
  69.3 131.7 %all-to-all-start = ((bf16[16,64,8,512]{3,2,1,0:T(8,128)(2,1)}), bf16[16,64,8,512]{3,2,1,0:T(8,128)(2,1)}, u32[]{:S(2)}, u32[]{:S(2)}) async-start(bf16[16,64,8,512]{3,2,1,0:T(8,128)(2,1)} %broadcast_select_fusion), calls=%async_computation | async-start | bytes 16777216 | tf_op jit(solution)/shard_map/all_to_all | solution.py:27
Sparse Core Ops, SparseCore 0:
  10.0 35.9 all-gather.1
where the time goes:
time: 219 us
  waiting for transfers between devices  159 us (73%)
  local copies, waits for them, and re-layouts  15.1 us (7%)
  between operations  13.4 us (6%)
  matrix products  13 us (6%)
  other arithmetic  11.8 us (5%)
  starting transfers between devices  6.71 us (3%)
    all_to_all x1, waiting for transfers between devices, body(): received = lax.all_to_all(send, 'col', 0, 0, tiled=True)  125 us
    all_gather x1, waiting for transfers between devices, body(): full_solved = lax.all_gather(own_solved, 'row', axis=1, tiled=True)  33.7 us
    select_n x1, other arithmetic, body(): jnp.where(present[:, None, None, None], products[position], jnp.zeros((),...  7.2 us
    gather x1, local copies, waits for them, and re-layouts, body(): products[position]  6.87 us
    all_to_all x1, starting transfers between devices, body(): received = lax.all_to_all(send, 'col', 0, 0, tiled=True)  6.71 us
    dot_general x1, matrix products, body(): jnp.einsum('sqb,siqm->ibm', onehot, received, preferred_element_type=jnp....  6.02 us
    dot_general x1, matrix products, body(): jnp.einsum('piw,qmw->piqm', own_solved, full_solved, preferred_element_ty...  4.73 us
    convert_element_type x1, local copies, waits for them, and re-layouts, body(): products = jnp.einsum('piw,qmw->piqm', own_solved, full_solved, preferred...  4.47 us
  transfers between devices with their start and end apart: 2, of which 2 were waited for; matrix products, arithmetic and copies ran while one was open for 1% of the time, Pallas kernels for 0%

commit v1 on v0

--- a/solution.py
+++ b/solution.py
@@ -2,6 +2,12 @@
 import jax.numpy as jnp
 from jax import lax
 from jax.sharding import PartitionSpec as P
+
+
+def in_order(blocks, dim):
+    blocks = jnp.moveaxis(blocks, 0, dim)
+    shape = blocks.shape
+    return blocks.reshape(*shape[:dim], shape[dim] * shape[dim + 1], *shape[dim + 2 :])
 
 
 def body(panel_blocks, factor_inverse, target_rows, owner_order, ancestor_rows):
@@ -13,7 +19,19 @@
     own_solved = jnp.einsum(
         "piw,vw->piv", panel_blocks[0], factor_inverse[0], preferred_element_type=jnp.float32
     ).astype(jnp.bfloat16)
-    full_solved = lax.all_gather(own_solved, "row", axis=1, tiled=True)
+    size = lax.axis_size("row")
+    pairs = [(i, (i + 1) % size) for i in range(size)]
+    back = [(b, a) for a, b in pairs]
+    lower, upper = ([], [])
+    for step in range(size - 1):
+        if step % 2 == 0:
+            lower.append(lax.ppermute(lower[-1] if lower else own_solved, "row", pairs))
+        else:
+            upper.append(lax.ppermute(upper[-1] if upper else own_solved, "row", back))
+    blocks = jnp.stack([*lower[::-1], own_solved, *upper])
+    shift = lax.axis_index("row") - len(lower)
+    blocks = blocks[(jnp.arange(size) - shift) % size]
+    full_solved = in_order(blocks, 1)
     products = jnp.einsum(
         "piw,qmw->piqm", own_solved, full_solved, preferred_element_type=jnp.float32
     ).astype(jnp.bfloat16)

time: 219 us -> 220 us (level)
  the two profiles are of different devices: /device:TPU:1 before, /device:TPU:97 now
where the time goes in v1:
time: 220 us
  waiting for transfers between devices  150 us (68%)
  local copies, waits for them, and re-layouts  29.3 us (13%)
  starting transfers between devices  18 us (8%)
  other arithmetic  11.9 us (5%)
  matrix products  10 us (5%)
    all_to_all x1, waiting for transfers between devices, body(): received = lax.all_to_all(send, 'col', 0, 0, tiled=True)  128 us
    ppermute x4, waiting for transfers between devices, body(): lower.append(lax.ppermute(lower[-1] if lower else own_solved, 'row', pairs))  21.2 us
    ppermute x4, starting transfers between devices, body(): lower.append(lax.ppermute(lower[-1] if lower else own_solved, 'row', pairs))  11.1 us
    select_n x1, other arithmetic, body(): jnp.where(present[:, None, None, None], products[position], jnp.zeros((),...  7.22 us
    unnamed x12, local copies, waits for them, and re-layouts  7.01 us
    all_to_all x1, starting transfers between devices, body(): received = lax.all_to_all(send, 'col', 0, 0, tiled=True)  6.93 us
    gather x1, local copies, waits for them, and re-layouts, body(): products[position]  6.88 us
    dot_general x1, matrix products, body(): jnp.einsum('sqb,siqm->ibm', onehot, received, preferred_element_type=jnp....  6.02 us
  transfers between devices with their start and end apart: 8, of which 6 were waited for; matrix products, arithmetic and copies ran while one was open for 4% of the time, Pallas kernels for 0%

profile of v1, /device:TPU:97, one launch (start us, length us, event | category | flops | bytes accessed | tf_op | source)
XLA Modules:
  0.0 219.7 jit_solution(12683726123276447445)
XLA Ops:
  0.0 0.0 copy-start
  0.0 1.0 copy-done
  1.0 1.5 convolution_convert_fusion.1
  2.6 0.0 collective-permute-start
  2.6 6.1 %collective-permute-done = bf16[8,64,512]{2,1,0:T(8,128)(2,1)S(1)} collective-permute-done((bf16[8,64,512]{2,1,0:T(8,128)(2,1)S(1)}, bf16[8,64,512]{2,1,0:T(8,128)(2,1)S(1)}, u32[]{:S(2)}, u32[]{:S(2)}) %collective-permute-start) | collective-permute-done | bytes 524320 | tf_op jit(solution)/shard_map/ppermute | solution.py:28
  8.7 3.7 %collective-permute-start.1 = (bf16[8,64,512]{2,1,0:T(8,128)(2,1)S(1)}, bf16[8,64,512]{2,1,0:T(8,128)(2,1)S(1)}, u32[]{:S(2)}, u32[]{:S(2)}) collective-permute-start(bf16[8,64,512]{2,1,0:T(8,128)(2,1)S(1)} %collective-permute-done), channel_id=1, source_target_pairs={{0,16},{16,32},{32,48},{48,64},{64,80},{80,96},{96,112},{112,0},{1... | collective-permute-start | bytes 1572872 | tf_op jit(solution)/shard_map/ppermute | solution.py:28
  12.4 0.0 collective-permute-start.4
  12.4 6.1 %collective-permute-done.1 = bf16[8,64,512]{2,1,0:T(8,128)(2,1)S(1)} collective-permute-done((bf16[8,64,512]{2,1,0:T(8,128)(2,1)S(1)}, bf16[8,64,512]{2,1,0:T(8,128)(2,1)S(1)}, u32[]{:S(2)}, u32[]{:S(2)}) %collective-permute-start.1) | collective-permute-done | bytes 524320 | tf_op jit(solution)/shard_map/ppermute | solution.py:28
  18.5 3.7 %collective-permute-start.2 = (bf16[8,64,512]{2,1,0:T(8,128)(2,1)S(1)}, bf16[8,64,512]{2,1,0:T(8,128)(2,1)S(1)}, u32[]{:S(2)}, u32[]{:S(2)}) collective-permute-start(bf16[8,64,512]{2,1,0:T(8,128)(2,1)S(1)} %collective-permute-done.1), channel_id=1, source_target_pairs={{0,16},{16,32},{32,48},{48,64},{64,80},{80,96},{96,112},{112,0},{1... | collective-permute-start | bytes 1572872 | tf_op jit(solution)/shard_map/ppermute | solution.py:28
  22.2 0.9 dynamic-slice_reduce_fusion
  23.1 0.7 fusion.6
  23.8 0.0 collective-permute-done.4
  23.8 0.0 collective-permute-start.5
  23.9 4.5 %collective-permute-done.2 = bf16[8,64,512]{2,1,0:T(8,128)(2,1)S(1)} collective-permute-done((bf16[8,64,512]{2,1,0:T(8,128)(2,1)S(1)}, bf16[8,64,512]{2,1,0:T(8,128)(2,1)S(1)}, u32[]{:S(2)}, u32[]{:S(2)}) %collective-permute-start.2) | collective-permute-done | bytes 524320 | tf_op jit(solution)/shard_map/ppermute | solution.py:28
  28.3 3.7 %collective-permute-start.3 = (bf16[8,64,512]{2,1,0:T(8,128)(2,1)S(1)}, bf16[8,64,512]{2,1,0:T(8,128)(2,1)S(1)}, u32[]{:S(2)}, u32[]{:S(2)}) collective-permute-start(bf16[8,64,512]{2,1,0:T(8,128)(2,1)S(1)} %collective-permute-done.2), channel_id=1, source_target_pairs={{0,16},{16,32},{32,48},{48,64},{64,80},{80,96},{96,112},{112,0},{1... | collective-permute-start | bytes 1572872 | tf_op jit(solution)/shard_map/ppermute | solution.py:28
  32.1 0.7 compare_reduce_fusion
  32.8 0.9 collective-permute-done.5
  33.7 0.0 collective-permute-start.6
  33.7 4.5 %collective-permute-done.3 = bf16[8,64,512]{2,1,0:T(8,128)(2,1)S(1)} collective-permute-done((bf16[8,64,512]{2,1,0:T(8,128)(2,1)S(1)}, bf16[8,64,512]{2,1,0:T(8,128)(2,1)S(1)}, u32[]{:S(2)}, u32[]{:S(2)}) %collective-permute-start.3) | collective-permute-done | bytes 524320 | tf_op jit(solution)/shard_map/ppermute | solution.py:28
  38.2 0.8 bitcast_dynamic-update-slice_fusion.7
  39.0 0.8 bitcast_dynamic-update-slice_fusion.6
  39.8 0.9 bitcast_dynamic-update-slice_fusion.5
  40.7 0.9 bitcast_dynamic-update-slice_fusion.4
  41.5 0.8 bitcast_dynamic-update-slice_fusion.3
  42.4 0.9 bitcast_dynamic-update-slice_fusion.2
  43.2 0.8 bitcast_dynamic-update-slice_fusion.1
  44.1 0.0 collective-permute-done.6
  44.1 0.8 bitcast_dynamic-update-slice_fusion
  44.9 5.0 %gather_fusion = bf16[8,8,64,512]{3,2,1,0:T(8,128)(2,1)} fusion(bf16[8,8,64,512]{3,2,1,0:T(8,128)(2,1)} %bitcast_dynamic-update-slice_fusion, s32[1024]{0:T(1024)S(1)} %pad_clamp_fusion.1), kind=kCustom, calls=%fused_computation | custom fusion | bytes 8388640 | tf_op jit(solution)/shard_map/gather | solution.py:33
  49.9 2.5 %copy.11 = bf16[8,8,64,512]{3,2,1,0:T(8,128)(2,1)S(1)} copy(bf16[8,8,64,512]{3,2,0,1:T(8,128)(2,1)} %bitcast.49) | data formatting | bytes 8388608 | tf_op jit(solution)/shard_map/transpose | solution.py:8
  52.3 2.5 %convolution_convert_fusion = bf16[8,64,8,512]{3,1,2,0:T(8,128)(2,1)S(1)} fusion(bf16[8,512,512,1]{2,1,0,3:T(8,128)(2,1)S(1)} %bitcast.50, bf16[8,64,512]{2,1,0:T(8,128)(2,1)S(1)} %convolution_convert_fusion.1), kind=kOutput, calls=%fused_computation.3 | convolution fusion | flops 2149580800 | bytes 8912896 | tf_op jit(solution)/shard_map/piw,qmw->piqm/dot_general | solution.py:35
  54.8 4.5 %copy.12 = bf16[8,64,8,512]{3,2,1,0:T(8,128)(2,1)} copy(bf16[8,64,8,512]{3,1,2,0:T(8,128)(2,1)S(1)} %convolution_convert_fusion) | data formatting | bytes 8388608 | tf_op jit(solution)/shard_map/convert_element_type | solution.py:37
  59.3 6.9 %gather_fusion.1 = bf16[16,64,8,512]{3,2,1,0:T(8,128)(2,1)} fusion(bf16[8,64,8,512]{3,2,1,0:T(8,128)(2,1)} %copy.12, s32[1024]{0:T(1024)S(1)} %pad_clamp_fusion), kind=kCustom, calls=%fused_computation.1 | custom fusion | bytes 16777280 | tf_op jit(solution)/shard_map/gather | solution.py:43
  66.2 7.2 %broadcast_select_fusion = bf16[16,64,8,512]{3,2,1,0:T(8,128)(2,1)} fusion(bf16[16,64,8,512]{3,2,1,0:T(8,128)(2,1)} %gather_fusion.1, pred[16]{0:T(512)(128)(4,1)S(1)} %compare_reduce_fusion), kind=kLoop, calls=%fused_computation.2 | loop fusion | flops 4194304 | bytes 16777232 | tf_op jit(solution)/shard_map/jit(_where)/select_n | solution.py:42
  73.4 0.0 copy-start.1
  73.4 6.9 %all-to-all-start = ((bf16[16,64,8,512]{3,2,1,0:T(8,128)(2,1)}), bf16[16,64,8,512]{3,2,1,0:T(8,128)(2,1)}, u32[]{:S(2)}, u32[]{:S(2)}) async-start(bf16[16,64,8,512]{3,2,1,0:T(8,128)(2,1)} %broadcast_select_fusion), calls=%async_computation | async-start | bytes 16777216 | tf_op jit(solution)/shard_map/all_to_all | solution.py:45
  80.3 0.0 copy-done.1
  80.4 0.1 copy.13
  80.4 128.4 %all-to-all-done = bf16[16,64,8,512]{3,2,1,0:T(8,128)(2,1)} async-done(((bf16[16,64,8,512]{3,2,1,0:T(8,128)(2,1)}), bf16[16,64,8,512]{3,2,1,0:T(8,128)(2,1)}, u32[]{:S(2)}, u32[]{:S(2)}) %all-to-all-start) | async-done | bytes 8388640 | tf_op jit(solution)/shard_map/all_to_all | solution.py:45
  208.8 6.0 %convolution_bitcast_fusion = f32[64,16,512]{2,1,0:T(8,128)} fusion(bf16[16,64,8,512]{3,2,1,0:T(8,128)(2,1)} %all-to-all-done, s32[16,8]{1,0:T(8,128)S(1)} %copy.13), kind=kOutput, calls=%fused_computation.4 | convolution fusion | flops 134219776 | bytes 10486272 | tf_op jit(solution)/shard_map/sqb,siqm->ibm/dot_general | solution.py:48
  214.8 1.7 reshape.72
  216.6 3.1 %sub.22 = f32[1,64,8192]{2,1,0:T(8,128)} subtract(f32[1,64,8192]{2,1,0:T(8,128)} %param.9, f32[1,64,8192]{2,1,0:T(8,128)S(1)} %reshape.72) | non-fusion elementwise | flops 524288 | bytes 6291456 | tf_op jit(solution)/shard_map/sub | solution.py:49
  (4 shorter events, 0.0 us)
Async XLA Ops:
  0.0 1.0 copy-start
  2.6 6.1 %collective-permute-start = (bf16[8,64,512]{2,1,0:T(8,128)(2,1)S(1)}, bf16[8,64,512]{2,1,0:T(8,128)(2,1)S(1)}, u32[]{:S(2)}, u32[]{:S(2)}) collective-permute-start(bf16[8,64,512]{2,1,0:T(8,128)(2,1)S(1)} %convolution_convert_fusion.1), channel_id=1, source_target_pairs={{0,16},{16,32},{32,48},{48,64},{64,80},{80,96},{96,112},{112,0},{1... | collective-permute-start | bytes 1572872 | tf_op jit(solution)/shard_map/ppermute | solution.py:28
  8.7 9.8 %collective-permute-start.1 = (bf16[8,64,512]{2,1,0:T(8,128)(2,1)S(1)}, bf16[8,64,512]{2,1,0:T(8,128)(2,1)S(1)}, u32[]{:S(2)}, u32[]{:S(2)}) collective-permute-start(bf16[8,64,512]{2,1,0:T(8,128)(2,1)S(1)} %collective-permute-done), channel_id=1, source_target_pairs={{0,16},{16,32},{32,48},{48,64},{64,80},{80,96},{96,112},{112,0},{1... | collective-permute-start | bytes 1572872 | tf_op jit(solution)/shard_map/ppermute | solution.py:28
  12.4 11.4 %collective-permute-start.4 = (bf16[8,64,512]{2,1,0:T(8,128)(2,1)S(1)}, bf16[8,64,512]{2,1,0:T(8,128)(2,1)S(1)}, u32[]{:S(2)}, u32[]{:S(2)}) collective-permute-start(bf16[8,64,512]{2,1,0:T(8,128)(2,1)S(1)} %convolution_convert_fusion.1), channel_id=1, source_target_pairs={{16,0},{32,16},{48,32},{64,48},{80,64},{96,80},{112,96},{0,112},{1... | collective-permute-start | bytes 1572872 | tf_op jit(solution)/shard_map/ppermute | solution.py:30
  18.5 9.8 %collective-permute-start.2 = (bf16[8,64,512]{2,1,0:T(8,128)(2,1)S(1)}, bf16[8,64,512]{2,1,0:T(8,128)(2,1)S(1)}, u32[]{:S(2)}, u32[]{:S(2)}) collective-permute-start(bf16[8,64,512]{2,1,0:T(8,128)(2,1)S(1)} %collective-permute-done.1), channel_id=1, source_target_pairs={{0,16},{16,32},{32,48},{48,64},{64,80},{80,96},{96,112},{112,0},{1... | collective-permute-start | bytes 1572872 | tf_op jit(solution)/shard_map/ppermute | solution.py:28
  23.8 9.8 %collective-permute-start.5 = (bf16[8,64,512]{2,1,0:T(8,128)(2,1)S(1)}, bf16[8,64,512]{2,1,0:T(8,128)(2,1)S(1)}, u32[]{:S(2)}, u32[]{:S(2)}) collective-permute-start(bf16[8,64,512]{2,1,0:T(8,128)(2,1)S(1)} %collective-permute-done.4), channel_id=1, source_target_pairs={{16,0},{32,16},{48,32},{64,48},{80,64},{96,80},{112,96},{0,112},{1... | collective-permute-start | bytes 1572872 | tf_op jit(solution)/shard_map/ppermute | solution.py:30
  28.3 9.8 %collective-permute-start.3 = (bf16[8,64,512]{2,1,0:T(8,128)(2,1)S(1)}, bf16[8,64,512]{2,1,0:T(8,128)(2,1)S(1)}, u32[]{:S(2)}, u32[]{:S(2)}) collective-permute-start(bf16[8,64,512]{2,1,0:T(8,128)(2,1)S(1)} %collective-permute-done.2), channel_id=1, source_target_pairs={{0,16},{16,32},{32,48},{48,64},{64,80},{80,96},{96,112},{112,0},{1... | collective-permute-start | bytes 1572872 | tf_op jit(solution)/shard_map/ppermute | solution.py:28
  33.7 10.4 %collective-permute-start.6 = (bf16[8,64,512]{2,1,0:T(8,128)(2,1)S(1)}, bf16[8,64,512]{2,1,0:T(8,128)(2,1)S(1)}, u32[]{:S(2)}, u32[]{:S(2)}) collective-permute-start(bf16[8,64,512]{2,1,0:T(8,128)(2,1)S(1)} %collective-permute-done.5), channel_id=1, source_target_pairs={{16,0},{32,16},{48,32},{64,48},{80,64},{96,80},{112,96},{0,112},{1... | collective-permute-start | bytes 1572872 | tf_op jit(solution)/shard_map/ppermute | solution.py:30
  73.4 6.9 %copy-start.1 = (s32[16,8]{0,1:T(8,128)S(1)}, s32[16,8]{0,1:T(8,128)}, u32[]{:S(2)}) copy-start(s32[16,8]{0,1:T(8,128)} %param.7) | copy-start | bytes 1540
  73.4 135.4 %all-to-all-start = ((bf16[16,64,8,512]{3,2,1,0:T(8,128)(2,1)}), bf16[16,64,8,512]{3,2,1,0:T(8,128)(2,1)}, u32[]{:S(2)}, u32[]{:S(2)}) async-start(bf16[16,64,8,512]{3,2,1,0:T(8,128)(2,1)} %broadcast_select_fusion), calls=%async_computation | async-start | bytes 16777216 | tf_op jit(solution)/shard_map/all_to_all | solution.py:45
